TPU v7x, 32 devices: a whole 2x2x4 slice. The times are simulated.
32 devices in a mesh: dp: 8 (over y, x, core), mp: 4 (over z).
Axes of the slice: x: 2, y: 2, z: 4, core: 2. Of those that a mesh axis runs over, the one named last changes fastest.
Arguments:
- tokens: bfloat16 [64, 256, 1024], P(('dp', 'mp')), may hold values from -6 to 6
- cotangent: bfloat16 [64, 256, 1024], P(('dp', 'mp')), may hold values from -6 to 6
- w_qkv: bfloat16 [3, 1024, 1024], P(None, None, 'mp'), may hold values from -0.1875 to 0.1875
- w_out: bfloat16 [1024, 1024], P('mp'), may hold values from -1 to 1
- w_up: bfloat16 [1024, 4096], P(None, 'mp'), may hold values from -0.1875 to 0.1875
- w_down: bfloat16 [4096, 1024], P('mp'), may hold values from -0.09375 to 0.09375
- w_mod: bfloat16 [1024, 6144], P('mp'), may hold values from -0.1875 to 0.1875
- b_mod: bfloat16 [6, 1024], replicated, may hold values from -3 to 3
- time_weight: bfloat16 [256, 1024], P(None, 'mp'), may hold values from -0.375 to 0.375
- class_table: bfloat16 [1000, 1024], P(None, 'mp'), may hold values from -6 to 6
- rel_table: bfloat16 [16, 961], P('mp'), may hold values from -5 to 5
- window_step: int32 [64], P('dp'), may hold values from 0 to 999
- window_label: int32 [64], P('dp'), may hold values from 0 to 999
- window_cols: int32 [64], P('dp'), may hold values from 0 to 16, as said below
Outputs:
- block_out: bfloat16 [64, 256, 1024], P(('dp', 'mp'))
- tokens_grad: bfloat16 [64, 256, 1024], P(('dp', 'mp'))
- w_qkv_grad: float32 [3, 1024, 1024], P(None, None, 'mp')
- w_out_grad: float32 [1024, 1024], P('mp')
- w_up_grad: float32 [1024, 4096], P(None, 'mp')
- w_down_grad: float32 [4096, 1024], P('mp')
- w_mod_grad: float32 [1024, 6144], P('mp')
- b_mod_grad: float32 [6, 1024], replicated
- time_weight_grad: float32 [256, 1024], P(None, 'mp')
- class_table_grad: float32 [1000, 1024], P(None, 'mp')
- rel_table_grad: float32 [16, 961], P('mp')
Inputs may be any that keep to these rules, and one draw needn't show every extreme that they name: `window_cols`: within each aligned block of 8 windows the used slots (nonzero entry) come first, two or more of them; some block is used in full. A used slot holds 16 or 8 valid columns, an unused one 0.
All inputs are finite; a program needn't handle non-finite values.
Results may differ from a plain program's by a relative error of at most 0.028.
Values may be sent and summed in bfloat16 or wider, within the bound.
No kernel may reach another device: no remote copies, remote signals or barrier semaphores. Data moves between devices by JAX's collectives and lax.ppermute only.
A program may use at most 192 MiB of HBM per device.

v0:
```python
import math
import jax
import jax.numpy as jnp
from jax import lax
from jax.sharding import PartitionSpec as P

HEAD_DIM = 64
WSIDE = 16
FREQ = 256
EPS = 1e-06
HIGH = lax.Precision.HIGHEST
MASKED = -1000000000.0


def exact(matrix_a, matrix_b):
    return jnp.dot(matrix_a, matrix_b, precision=HIGH, preferred_element_type=jnp.float32)


def layer_norm(field):
    center = field - jnp.mean(field, axis=-1, keepdims=True)
    spread = jnp.mean(center * center, axis=-1, keepdims=True)
    return center * lax.rsqrt(spread + EPS)


def modulate(field, scale_part, shift_part):
    return layer_norm(field) * (1.0 + scale_part) + shift_part


def gelu_tanh(field):
    return jax.nn.gelu(field, approximate=True)


def step_features(step_ids, half_width):
    frequency = jnp.exp(-math.log(10000.0) * jnp.arange(half_width, dtype=jnp.float32) / half_width)
    angles = step_ids.astype(jnp.float32)[:, None] * frequency[None, :]
    return jnp.concatenate([jnp.cos(angles), jnp.sin(angles)], axis=1)


def offset_table(window_side):
    offsets = jnp.arange(window_side, dtype=jnp.int32)
    offset_diff = offsets[:, None] - offsets[None, :] + window_side - 1
    return (
        offset_diff[None] == jnp.arange(2 * window_side - 1, dtype=jnp.int32)[:, None, None]
    ).astype(jnp.float32)


def make_scores(queries, keys, rel_bias, keep_keys, score_scale):
    raw_scores = (
        jnp.einsum("wihd,wjhd->whij", queries, keys, preferred_element_type=jnp.float32)
        * score_scale
        + rel_bias[None]
    )
    return jnp.where(keep_keys[:, None, None, :], raw_scores, MASKED)


def per_device(
    tokens,
    cotangent,
    w_qkv,
    w_out,
    w_up,
    w_down,
    w_mod,
    b_mod,
    time_weight,
    class_table,
    rel_table,
    window_step,
    window_label,
    window_cols,
):
    own_count, win_tok, width = tokens.shape
    group_size = window_step.shape[0]
    local_heads = w_out.shape[0] // HEAD_DIM
    score_scale = HEAD_DIM ** (-0.5)
    first_own = lax.axis_index("mp") * own_count
    features = step_features(window_step, FREQ // 2).astype(jnp.bfloat16)
    classes = jnp.arange(class_table.shape[0], dtype=jnp.int32)
    onehot = (window_label[:, None] == classes[None, :]).astype(jnp.bfloat16)
    cond_pre = jnp.dot(features, time_weight, preferred_element_type=jnp.float32) + jnp.dot(
        onehot, class_table, preferred_element_type=jnp.float32
    )
    condition = jax.nn.silu(cond_pre).astype(jnp.bfloat16)
    partial_mod = jnp.dot(condition, w_mod, preferred_element_type=jnp.float32)
    modulation = (
        lax.psum(partial_mod, "mp").reshape(group_size, 6, width) + b_mod.astype(jnp.float32)[None]
    )
    own_mod = lax.dynamic_slice_in_dim(modulation, first_own, own_count, 0)
    shift_attn, scale_attn, gate_attn, shift_mlp, scale_mlp, gate_mlp = [
        own_mod[:, column][:, None, :] for column in range(6)
    ]
    token_cols = jnp.arange(win_tok, dtype=jnp.int32) % WSIDE
    keep_keys = token_cols[None, :] < window_cols[:, None]
    keep_rows = lax.dynamic_slice_in_dim(keep_keys, first_own, own_count, 0)[:, :, None]
    rel_span = 2 * WSIDE - 1
    offset_pick = offset_table(WSIDE)
    rel_grid = rel_table.astype(jnp.float32).reshape(local_heads, rel_span, rel_span)
    half_bias = jnp.einsum("ayz,hab->hyzb", offset_pick, rel_grid, precision=HIGH)
    rel_bias = jnp.einsum("hyzb,bxw->hyxzw", half_bias, offset_pick, precision=HIGH).reshape(
        local_heads, win_tok, win_tok
    )
    inputs = tokens.astype(jnp.float32)
    normed_attn = modulate(inputs, scale_attn, shift_attn).astype(jnp.bfloat16)
    gathered_attn = lax.all_gather(normed_attn, "mp", axis=0, tiled=True)
    projected = jnp.einsum(
        "wtd,kde->kwte", gathered_attn, w_qkv, preferred_element_type=jnp.float32
    ).astype(jnp.bfloat16)
    split_shape = (group_size, win_tok, local_heads, HEAD_DIM)
    queries = projected[0].reshape(split_shape)
    keys = projected[1].reshape(split_shape)
    values = projected[2].reshape(split_shape)
    scores = make_scores(queries, keys, rel_bias, keep_keys, score_scale)
    row_max = jnp.max(scores, axis=-1, keepdims=True)
    log_total = row_max + jnp.log(jnp.sum(jnp.exp(scores - row_max), axis=-1, keepdims=True))
    probs_low = jnp.exp(scores - log_total).astype(jnp.bfloat16)
    attended = (
        jnp.einsum("whij,wjhd->wihd", probs_low, values, preferred_element_type=jnp.float32)
        .astype(jnp.bfloat16)
        .reshape(group_size, win_tok, local_heads * HEAD_DIM)
    )
    row_block = attended
    branch = lax.psum_scatter(
        jnp.einsum("wte,ed->wtd", row_block, w_out, preferred_element_type=jnp.float32).astype(
            jnp.bfloat16
        ),
        "mp",
        scatter_dimension=0,
        tiled=True,
    ).astype(jnp.float32)
    middle = inputs + gate_attn * branch
    normed_mlp = modulate(middle, scale_mlp, shift_mlp).astype(jnp.bfloat16)
    gathered_mlp = lax.all_gather(normed_mlp, "mp", axis=0, tiled=True)
    hidden_pre = jnp.einsum("wtd,df->wtf", gathered_mlp, w_up, preferred_element_type=jnp.float32)
    activation = gelu_tanh(hidden_pre).astype(jnp.bfloat16)
    row_block = activation
    mlp_out = lax.psum_scatter(
        jnp.einsum("wtf,fd->wtd", row_block, w_down, preferred_element_type=jnp.float32).astype(
            jnp.bfloat16
        ),
        "mp",
        scatter_dimension=0,
        tiled=True,
    ).astype(jnp.float32)
    block_out = jnp.where(keep_rows, middle + gate_mlp * mlp_out, 0.0).astype(jnp.bfloat16)
    grad_rows = jnp.where(keep_rows, cotangent.astype(jnp.float32), 0.0)
    d_gate_mlp = jnp.sum(grad_rows * mlp_out, axis=1)
    d_mlp = (gate_mlp * grad_rows).astype(jnp.bfloat16)
    d_mlp_all = lax.all_gather(d_mlp, "mp", axis=0, tiled=True)
    normed_again = lax.all_gather(normed_mlp, "mp", axis=0, tiled=True)
    pre_again = jnp.einsum("wtd,df->wtf", normed_again, w_up, preferred_element_type=jnp.float32)
    act_again = gelu_tanh(pre_again).astype(jnp.bfloat16)
    w_down_grad = jnp.einsum(
        "wtf,wtd->fd", act_again, d_mlp_all, preferred_element_type=jnp.float32
    )
    d_act = jnp.einsum("wtd,fd->wtf", d_mlp_all, w_down, preferred_element_type=jnp.float32)
    d_hidden = jax.vjp(gelu_tanh, pre_again)[1](d_act)[0].astype(jnp.bfloat16)
    w_up_grad = jnp.einsum(
        "wtd,wtf->df", normed_again, d_hidden, preferred_element_type=jnp.float32
    )
    row_block = d_hidden
    d_normed_mlp = lax.psum_scatter(
        jnp.einsum("wtf,df->wtd", row_block, w_up, preferred_element_type=jnp.float32),
        "mp",
        scatter_dimension=0,
        tiled=True,
    )
    pull_mlp = jax.vjp(modulate, middle, scale_mlp, shift_mlp)[1]
    d_middle_norm, d_scale_mlp, d_shift_mlp = pull_mlp(d_normed_mlp)
    d_middle = grad_rows + d_middle_norm
    d_gate_attn = jnp.sum(d_middle * branch, axis=1)
    d_branch = (gate_attn * d_middle).astype(jnp.bfloat16)
    d_branch_all = lax.all_gather(d_branch, "mp", axis=0, tiled=True)
    w_out_grad = jnp.einsum(
        "wte,wtd->ed", attended, d_branch_all, preferred_element_type=jnp.float32
    )
    d_attended = (
        jnp.einsum("wtd,ed->wte", d_branch_all, w_out, preferred_element_type=jnp.float32)
        .astype(jnp.bfloat16)
        .reshape(split_shape)
    )
    probs_back = jnp.exp(make_scores(queries, keys, rel_bias, keep_keys, score_scale) - log_total)
    d_probs = jnp.einsum("wihd,wjhd->whij", d_attended, values, preferred_element_type=jnp.float32)
    d_values = jnp.einsum(
        "whij,wihd->wjhd",
        probs_back.astype(jnp.bfloat16),
        d_attended,
        preferred_element_type=jnp.float32,
    ).astype(jnp.bfloat16)
    row_delta = jnp.sum(probs_back * d_probs, axis=-1, keepdims=True)
    d_scores = (probs_back * (d_probs - row_delta)).astype(jnp.bfloat16)
    d_queries = (
        jnp.einsum("whij,wjhd->wihd", d_scores, keys, preferred_element_type=jnp.float32)
        * score_scale
    ).astype(jnp.bfloat16)
    d_keys = (
        jnp.einsum("whij,wihd->wjhd", d_scores, queries, preferred_element_type=jnp.float32)
        * score_scale
    ).astype(jnp.bfloat16)
    d_bias = jnp.sum(d_scores, axis=0, dtype=jnp.float32).reshape(
        local_heads, WSIDE, WSIDE, WSIDE, WSIDE
    )
    d_half = jnp.einsum("hyxzw,bxw->hyzb", d_bias, offset_pick, precision=HIGH)
    rel_table_grad = jnp.einsum("hyzb,ayz->hab", d_half, offset_pick, precision=HIGH).reshape(
        local_heads, rel_span * rel_span
    )
    d_projected = jnp.stack([d_queries, d_keys, d_values]).reshape(
        3, group_size, win_tok, local_heads * HEAD_DIM
    )
    w_qkv_grad = jnp.einsum(
        "wtd,kwte->kde", gathered_attn, d_projected, preferred_element_type=jnp.float32
    )
    row_block = d_projected
    d_normed_attn = lax.psum_scatter(
        jnp.einsum("kwte,kde->wtd", row_block, w_qkv, preferred_element_type=jnp.float32).astype(
            jnp.bfloat16
        ),
        "mp",
        scatter_dimension=0,
        tiled=True,
    ).astype(jnp.float32)
    pull_attn = jax.vjp(modulate, inputs, scale_attn, shift_attn)[1]
    d_inputs_norm, d_scale_attn, d_shift_attn = pull_attn(d_normed_attn)
    tokens_grad = (d_middle + d_inputs_norm).astype(jnp.bfloat16)
    d_mod_own = jnp.stack(
        [
            d_shift_attn[:, 0],
            d_scale_attn[:, 0],
            d_gate_attn,
            d_shift_mlp[:, 0],
            d_scale_mlp[:, 0],
            d_gate_mlp,
        ],
        axis=1,
    ).reshape(own_count, 6 * width)
    d_modulation = lax.all_gather(d_mod_own.astype(jnp.bfloat16), "mp", axis=0, tiled=True).astype(
        d_mod_own.dtype
    )
    d_condition = exact(d_modulation, w_mod.T)
    d_cond_pre = jax.vjp(jax.nn.silu, cond_pre)[1](d_condition)[0]
    time_weight_grad = exact(features.astype(jnp.float32).T, d_cond_pre)
    class_table_grad = exact(onehot.astype(jnp.float32).T, d_cond_pre)
    w_mod_grad = exact(condition.astype(jnp.float32).T, d_modulation)
    b_mod_grad = jnp.sum(d_modulation, axis=0).reshape(6, width)
    (
        w_qkv_grad,
        w_out_grad,
        w_up_grad,
        w_down_grad,
        w_mod_grad,
        b_mod_grad,
        time_weight_grad,
        class_table_grad,
        rel_table_grad,
    ) = lax.psum(
        (
            w_qkv_grad,
            w_out_grad,
            w_up_grad,
            w_down_grad,
            w_mod_grad,
            b_mod_grad,
            time_weight_grad,
            class_table_grad,
            rel_table_grad,
        ),
        "dp",
    )
    return (
        block_out,
        tokens_grad,
        w_qkv_grad,
        w_out_grad,
        w_up_grad,
        w_down_grad,
        w_mod_grad,
        b_mod_grad,
        time_weight_grad,
        class_table_grad,
        rel_table_grad,
    )


def solution(mesh):
    return jax.shard_map(
        per_device,
        mesh=mesh,
        in_specs=(
            P(("dp", "mp"), None, None),
            P(("dp", "mp"), None, None),
            P(None, None, "mp"),
            P("mp", None),
            P(None, "mp"),
            P("mp", None),
            P("mp", None),
            P(),
            P(None, "mp"),
            P(None, "mp"),
            P("mp", None),
            P("dp"),
            P("dp"),
            P("dp"),
        ),
        out_specs=(
            P(("dp", "mp"), None, None),
            P(("dp", "mp"), None, None),
            P(None, None, "mp"),
            P("mp", None),
            P(None, "mp"),
            P("mp", None),
            P("mp", None),
            P(),
            P(None, "mp"),
            P(None, "mp"),
            P("mp", None),
        ),
        check_vma=False,
    )
```

profile of v0, /device:TPU:0, one launch (start us, length us, event | category | flops | bytes accessed | tf_op | source)
XLA Modules:
  0.0 1149.7 jit_solution(5632088591709699951)
XLA Ops:
  11.8 1.4 convert_reduce_fusion.1
  13.2 1.6 fusion.28
  14.9 34.8 %all-reduce.5.cloned.1.call-done = f32[8,6,1024]{2,0,1:T(8,128)} async-done(((f32[8,6,1024]{2,0,1:T(8,128)}), f32[8,6,1024]{2,0,1:T(8,128)}) %all-reduce.5.cloned.1.call-update) | async-done | bytes 196624 | tf_op jit(solution)/shard_map/psum | solution.py:86
  50.6 2.7 fusion.21
  54.1 5.6 convolution_bitcast_fusion
  59.8 12.0 %copy.103 = f32[4,16,16,16,16]{2,1,4,3,0:T(8,128)} copy(f32[4,16,16,16,16]{3,4,1,0,2:T(8,128)} %convolution_bitcast_fusion) | data formatting | bytes 2097152 | tf_op jit(solution)/shard_map/add | solution.py:49
  71.8 7.0 reshape.213
  78.9 55.0 %all-gather.6.cloned.1.call-done = bf16[8,256,1024]{2,1,0:T(8,128)(2,1)} async-done(((bf16[2,256,1024]{2,1,0:T(8,128)(2,1)}), bf16[8,256,1024]{2,1,0:T(8,128)(2,1)}) %all-gather.6.cloned.1.call-update) | async-done | bytes 4194320 | tf_op jit(solution)/shard_map/all_gather | solution.py:104
  133.9 6.1 convert_bitcast_fusion
  141.4 2.9 fusion.83
  144.3 1.7 exponential_reduce_fusion
  146.0 1.5 copy-done.1
  147.5 1.4 convolution_convert_fusion.4
  149.9 3.3 convolution_convert_fusion.1
  153.3 75.4 %reduce-scatter.5.cloned.1.call-done = bf16[2,256,1024]{2,1,0:T(8,128)(2,1)} async-done(((bf16[8,256,1024]{2,1,0:T(8,128)(2,1)}), bf16[2,256,1024]{2,1,0:T(8,128)(2,1)}) %reduce-scatter.5.cloned.1.call-update) | async-done | bytes 1048592 | tf_op jit(solution)/shard_map/reduce_scatter | solution.py:122
  228.7 2.1 fusion.40
  230.8 2.1 multiply_reduce_fusion.3
  233.0 1.6 add_convert_fusion.1
  234.7 2.5 multiply_convert_fusion.5
  237.2 78.7 %all-gather.8.cloned.1.call-done = bf16[8,256,1024]{2,1,0:T(8,128)(2,1)} async-done(((bf16[2,256,1024]{2,1,0:T(8,128)(2,1)}), bf16[8,256,1024]{2,1,0:T(8,128)(2,1)}) %all-gather.8.cloned.1.call-update) | async-done | bytes 4194320 | tf_op jit(solution)/shard_map/all_gather | solution.py:132
  316.0 10.9 fusion.34
  326.9 70.4 %all-gather.10.cloned.1.call-done = bf16[8,256,1024]{2,1,0:T(8,128)(2,1)} async-done(((bf16[2,256,1024]{2,1,0:T(8,128)(2,1)}), bf16[8,256,1024]{2,1,0:T(8,128)(2,1)}) %all-gather.10.cloned.1.call-update) | async-done | bytes 4194320 | tf_op jit(solution)/shard_map/all_gather | solution.py:148
  397.2 12.8 %fusion.6 = bf16[8,256,1024]{2,1,0:T(8,128)(2,1)S(1)} fusion(f32[8,256,1024]{2,1,0:T(8,128)} %fusion.34, bf16[8,256,1024]{2,1,0:T(8,128)(2,1)} %all-gather.10.cloned.1.call-done, bf16[1024,1024]{1,0:T(8,128)(2,1)} %param.19), kind=kOutput, calls=%fused_computation.8 | convolution fusion | flops 4336910336 | bytes 18874368 | tf_op jit(solution)/shard_map/wtd,fd->wtf/dot_general | solution.py:155
  410.0 2.0 copy-done.35
  412.0 7.0 fusion.32
  419.1 143.2 %reduce-scatter.9.cloned.1.call-done = f32[2,256,1024]{2,1,0:T(8,128)} async-done(((f32[8,256,1024]{2,1,0:T(8,128)}), f32[2,256,1024]{2,1,0:T(8,128)}) %reduce-scatter.9.cloned.1.call-update) | async-done | bytes 2097168 | tf_op jit(solution)/shard_map/reduce_scatter | solution.py:161
  562.3 3.3 multiply_reduce_fusion.1
  566.7 1.3 copy-done.6
  568.1 1.4 multiply_convert_fusion.4
  569.6 81.5 %all-gather.12.cloned.1.call-done = bf16[8,256,1024]{2,1,0:T(8,128)(2,1)} async-done(((bf16[2,256,1024]{2,1,0:T(8,128)(2,1)}), bf16[8,256,1024]{2,1,0:T(8,128)(2,1)}) %all-gather.12.cloned.1.call-update) | async-done | bytes 4194320 | tf_op jit(solution)/shard_map/all_gather | solution.py:172
  651.0 3.7 convolution_convert_fusion.3
  654.8 6.0 convolution_convert_fusion.2
  660.8 2.5 multiply_reduce_fusion
  663.3 3.9 convert_reduce_fusion
  667.2 2.4 multiply_convert_fusion.2
  669.5 1.8 multiply_convert_fusion.3
  671.4 2.3 copy.79
  673.6 2.2 copy.77
  675.9 2.3 copy.78
  678.1 7.8 bitcast_convert_fusion
  686.0 11.5 %convolution_convert_fusion = bf16[8,256,1024]{2,1,0:T(8,128)(2,1)} fusion(bf16[1024,1024]{1,0:T(8,128)(2,1)} %param.19, f32[8,256,1024]{2,1,0:T(8,128)} %fusion.34), kind=kOutput, calls=%fused_computation.34 | convolution fusion | flops 4315938816 | bytes 14680064 | tf_op jit(solution)/shard_map/wtf,fd->wtd/dot_general | solution.py:137
  697.8 10.2 convolution_bitcast_fusion.2
  708.1 11.2 convolution_bitcast_fusion.1
  719.3 2.3 convolution_bitcast_fusion.3
  722.8 5.5 fusion.36
  728.3 33.1 %reduce-scatter.11.cloned.1.call-done = bf16[2,256,1024]{2,1,0:T(8,128)(2,1)} async-done(((bf16[8,256,1024]{2,1,0:T(8,128)(2,1)}), bf16[2,256,1024]{2,1,0:T(8,128)(2,1)}) %reduce-scatter.11.cloned.1.call-update) | async-done | bytes 1048592 | tf_op jit(solution)/shard_map/reduce_scatter | solution.py:213
  761.4 1.4 reduce
  762.9 2.1 fusion.29
  765.0 2.7 fusion.27
  767.7 74.0 %reduce-scatter.7.cloned.1.call-done = bf16[2,256,1024]{2,1,0:T(8,128)(2,1)} async-done(((bf16[8,256,1024]{2,1,0:T(8,128)(2,1)}), bf16[2,256,1024]{2,1,0:T(8,128)(2,1)}) %reduce-scatter.7.cloned.1.call-update) | async-done | bytes 1048592 | tf_op jit(solution)/shard_map/reduce_scatter | solution.py:136
  841.6 5.2 fusion.26
  847.0 13.8 %all-gather = bf16[4,2,6144]{2,1,0:T(2,128)(2,1)S(1)} all-gather(bf16[1,2,6144]{2,1,0:T(2,128)(2,1)S(1)} %bitcast.178), channel_id=1, replica_groups=mesh['dp'=8,'mp'=4] {'mp'}, dimensions={0}, use_global_device_ids=true | all-gather | bytes 122880 | tf_op jit(solution)/shard_map/all_gather | solution.py:235
  862.8 1.7 fusion.60
  864.4 3.7 fusion.77
  869.0 6.2 reshape.189
  875.2 6.8 convolution_bitcast_fusion.5
  882.7 25.6 %all-reduce = (f32[6,1024]{1,0:T(8,128)}, f32[4,961]{1,0:T(4,128)}) all-reduce(f32[6,1024]{1,0:T(8,128)S(1)} %reshape.188, f32[4,961]{1,0:T(4,128)S(1)} %reshape.190), channel_id=1, replica_groups=mesh['dp'=8,'mp'=4] {'dp'}, use_global_device_ids=true, to_apply=%region_28.29 | all-reduce | flops 9988 | bytes 79904 | tf_op jit(solution)/shard_map/psum | solution.py:254
  908.3 215.6 %all-reduce.7.cloned.1.call-done = (f32[3,1024,256]{1,2,0:T(8,128)}, f32[256,1024]{1,0:T(8,128)}, f32[1024,1024]{1,0:T(8,128)}, f32[1024,1024]{1,0:T(8,128)}, f3...) async-done(((f32[3,1024,256]{1,2,0:T(8,128)}, f32[256,1024]{1,0:T(8,128)}, f32[1024,1024]{1,0:T(8,128)}, f32[1024,1024]{1,0:T(8,128)}, ...) | async-done | bytes 20160528 | tf_op jit(solution)/shard_map/psum | solution.py:254
  1123.8 3.5 copy.85
  1127.4 2.3 copy.124
  1129.7 5.1 copy.125
  1134.8 2.1 copy.126
  1136.9 1.4 slice-done.3
  1138.3 2.7 copy.127
  (140 shorter events, 17.0 us)
Async XLA Ops:
  7.2 3.3 copy-start
  7.2 42.5 %all-reduce.5.cloned.1.call-start = ((), (), s32[]{:S(2)}) async-start(), calls=%async_computation.4 | async-start | bytes 393216 | tf_op jit(solution)/shard_map/psum | solution.py:86
  8.2 6.7 copy-start.27
  11.7 41.7 %copy-start.28 = (bf16[4,961]{1,0:T(4,128)(2,1)S(1)}, bf16[4,961]{1,0:T(4,128)(2,1)}, u32[]{:S(2)}) copy-start(bf16[4,961]{1,0:T(4,128)(2,1)} %param.24) | copy-start | bytes 23068
  11.7 122.2 %all-gather.6.cloned.1.call-start = ((), (), s32[]{:S(2)}) async-start(), calls=%async_computation.5 | async-start | bytes 5242880 | tf_op jit(solution)/shard_map/all_gather | solution.py:104
  53.3 175.4 %reduce-scatter.5.cloned.1.call-start = ((), (), s32[]{:S(2)}) async-start(), calls=%async_computation.6 | async-start | bytes 5242880 | tf_op jit(solution)/shard_map/reduce_scatter | solution.py:122
  53.5 0.6 copy-start.25
  71.8 7.0 copy-start.30
  140.0 1.4 copy-start.15
  140.3 4.0 copy-start.7
  140.3 4.0 copy-start.12
  140.3 5.7 copy-start.9
  144.3 3.2 copy-start.1
  147.5 2.4 copy-start.23
  149.0 1.0 copy-start.17
  153.3 162.7 %all-gather.8.cloned.1.call-start = ((), (), s32[]{:S(2)}) async-start(), calls=%async_computation.7 | async-start | bytes 5242880 | tf_op jit(solution)/shard_map/all_gather | solution.py:132
  228.7 4.2 copy-start.2
  228.7 4.2 copy-start.4
  234.6 162.6 %all-gather.10.cloned.1.call-start = ((), (), s32[]{:S(2)}) async-start(), calls=%async_computation.9 | async-start | bytes 5242880 | tf_op jit(solution)/shard_map/all_gather | solution.py:148
  237.2 325.1 %reduce-scatter.9.cloned.1.call-start = ((), (), s32[]{:S(2)}) async-start(), calls=%async_computation.10 | async-start | bytes 10485760 | tf_op jit(solution)/shard_map/reduce_scatter | solution.py:161
  397.2 14.8 %copy-start.34 = (bf16[1024,1024]{1,0:T(8,128)(2,1)S(1)}, bf16[1024,1024]{1,0:T(8,128)(2,1)}, u32[]{:S(2)}) copy-start(bf16[1024,1024]{1,0:T(8,128)(2,1)} %param.18) | copy-start | bytes 6291460
  410.0 2.0 copy-start.35
  419.0 232.0 %all-gather.12.cloned.1.call-start = ((), (), s32[]{:S(2)}) async-start(), calls=%async_computation.11 | async-start | bytes 5242880 | tf_op jit(solution)/shard_map/all_gather | solution.py:172
  562.3 3.3 copy-start.3
  562.3 3.4 copy-start.5
  562.3 3.5 copy-start.14
  565.8 2.3 copy-start.11
  566.7 1.4 copy-start.6
  569.5 191.9 %reduce-scatter.11.cloned.1.call-start = ((), (), s32[]{:S(2)}) async-start(), calls=%async_computation.12 | async-start | bytes 5242880 | tf_op jit(solution)/shard_map/reduce_scatter | solution.py:213
  651.0 9.7 slice-start
  654.8 6.0 slice-start.1
  654.8 6.0 copy-start.10
  663.3 3.9 copy-start.13
  667.2 2.4 copy-start.8
  686.0 155.7 %reduce-scatter.7.cloned.1.call-start = ((), (), s32[]{:S(2)}) async-start(), calls=%async_computation.8 | async-start | bytes 5242880 | tf_op jit(solution)/shard_map/reduce_scatter | solution.py:136
  697.6 426.2 %all-reduce.7.cloned.1.call-start = ((), (), s32[]{:S(2)}) async-start(), calls=%async_computation.13 | async-start | bytes 40321024 | tf_op jit(solution)/shard_map/psum | solution.py:254
  697.8 10.2 copy-start.32
  708.1 11.2 copy-start.18
  708.1 11.2 copy-start.33
  719.3 2.3 copy-start.19
  719.3 2.3 copy-start.20
  719.3 2.3 copy-start.21
  719.3 3.6 copy-start.31
  846.9 15.9 %copy-start.29 = (s32[8]{0:T(128)S(1)}, s32[8]{0:T(128)}, u32[]{:S(2)}) copy-start(s32[8]{0:T(128)} %param.26) | copy-start | bytes 100
  868.2 0.7 copy-start.26
  1129.7 5.1 copy-start.16
  1129.7 7.2 slice-start.2
  1134.8 3.5 slice-start.3
  1138.3 2.7 copy-start.24
  1138.3 3.4 copy-start.22
Sparse Core Ops, SparseCore 0:
  11.9 37.7 all-reduce.4
  53.5 80.3 all-gather.5
  153.4 75.2 reduce-scatter.4
  234.7 81.2 all-gather.7
  318.0 79.2 all-gather.9
  419.2 143.0 reduce-scatter.8
  569.6 81.3 all-gather.11
  686.1 75.2 reduce-scatter.10
  764.3 77.2 reduce-scatter.6
  868.3 255.4 all-reduce.6
where the time goes:
time: 1160 us; the launch traced here: 1150 us
  waiting for transfers between devices  862 us (74%)
  matrix products  133 us (11%)
  local copies, waits for them, and re-layouts  60.8 us (5%)
  blocking collectives  39.4 us (3%)
  other arithmetic  38.9 us (3%)
  between operations  14.9 us (1%)
    psum x1, waiting for transfers between devices, per_device(): lax.psum((w_qkv_grad, w_out_grad, w_up_grad, w_down_grad, w_mod_grad, b_m...  216 us
    reduce_scatter x1, waiting for transfers between devices, per_device(): lax.psum_scatter(jnp.einsum('wtf,df->wtd', row_block, w_up, preferred_ele...  143 us
    all_gather x1, waiting for transfers between devices, per_device(): d_branch_all = lax.all_gather(d_branch, 'mp', axis=0, tiled=True)  81.5 us
    all_gather x1, waiting for transfers between devices, per_device(): gathered_mlp = lax.all_gather(normed_mlp, 'mp', axis=0, tiled=True)  78.7 us
    reduce_scatter x1, waiting for transfers between devices, per_device(): lax.psum_scatter(jnp.einsum('wte,ed->wtd', row_block, w_out, preferred_el...  75.4 us
    reduce_scatter x1, waiting for transfers between devices, per_device(): lax.psum_scatter(jnp.einsum('wtf,fd->wtd', row_block, w_down, preferred_e...  74 us
    all_gather x1, waiting for transfers between devices, per_device(): d_mlp_all = lax.all_gather(d_mlp, 'mp', axis=0, tiled=True)  70.4 us
    all_gather x1, waiting for transfers between devices, per_device(): gathered_attn = lax.all_gather(normed_attn, 'mp', axis=0, tiled=True)  55 us
  transfers between devices with their start and end apart: 10, of which 10 were waited for; matrix products, arithmetic and copies ran while one was open for 9% of the time, Pallas kernels for 0%

commit v1 on v0

--- a/solution.py
+++ b/solution.py
@@ -69,6 +69,10 @@
     window_label,
     window_cols,
 ):
+
+    def clear_samples_all(arr, axis_tag="mp"):
+        return jnp.sum(lax.all_gather(arr, axis_tag), 0)
+
     own_count, win_tok, width = tokens.shape
     group_size = window_step.shape[0]
     local_heads = w_out.shape[0] // HEAD_DIM
@@ -83,7 +87,8 @@
     condition = jax.nn.silu(cond_pre).astype(jnp.bfloat16)
     partial_mod = jnp.dot(condition, w_mod, preferred_element_type=jnp.float32)
     modulation = (
-        lax.psum(partial_mod, "mp").reshape(group_size, 6, width) + b_mod.astype(jnp.float32)[None]
+        clear_samples_all(partial_mod).reshape(group_size, 6, width)
+        + b_mod.astype(jnp.float32)[None]
     )
     own_mod = lax.dynamic_slice_in_dim(modulation, first_own, own_count, 0)
     shift_attn, scale_attn, gate_attn, shift_mlp, scale_mlp, gate_mlp = [

time: 1160 us -> 1140 us (0.983)
  waiting for transfers between devices: 862 us -> 826 us
  blocking collectives: 39.4 us -> 61 us
    psum x1 -> x0, waiting for transfers between devices: 34.8 us -> none  [per_device(): lax.psum(partial_mod, 'mp').reshape(group_size, 6, width)]
    all_gather x0 -> x1, blocking collectives: none -> 21.4 us  [clear_samples_all(): return jnp.sum(lax.all_gather(arr, axis_tag), 0)]
    unnamed x93 -> x91, local copies, waits for them, and re-layouts: 28.4 us -> 28.4 us
  transfers between devices with their start and end apart: 10 -> 9, of which waited for: 10 -> 9; matrix products, arithmetic and copies ran while one was open for 9% -> 9% of each run, Pallas kernels for 0% -> 0%
where the time goes in v1:
time: 1140 us; the launch traced here: 1130 us
  waiting for transfers between devices  826 us (72%)
  matrix products  133 us (12%)
  blocking collectives  61 us (5%)
  local copies, waits for them, and re-layouts  60.7 us (5%)
  other arithmetic  38.9 us (3%)
  between operations  14.6 us (1%)
    psum x1, waiting for transfers between devices, per_device(): lax.psum((w_qkv_grad, w_out_grad, w_up_grad, w_down_grad, w_mod_grad, b_m...  215 us
    reduce_scatter x1, waiting for transfers between devices, per_device(): lax.psum_scatter(jnp.einsum('wtf,df->wtd', row_block, w_up, preferred_ele...  143 us
    all_gather x1, waiting for transfers between devices, per_device(): d_branch_all = lax.all_gather(d_branch, 'mp', axis=0, tiled=True)  81.5 us
    all_gather x1, waiting for transfers between devices, per_device(): gathered_mlp = lax.all_gather(normed_mlp, 'mp', axis=0, tiled=True)  78.7 us
    reduce_scatter x1, waiting for transfers between devices, per_device(): lax.psum_scatter(jnp.einsum('wte,ed->wtd', row_block, w_out, preferred_el...  75.4 us
    reduce_scatter x1, waiting for transfers between devices, per_device(): lax.psum_scatter(jnp.einsum('wtf,fd->wtd', row_block, w_down, preferred_e...  73.9 us
    all_gather x1, waiting for transfers between devices, per_device(): d_mlp_all = lax.all_gather(d_mlp, 'mp', axis=0, tiled=True)  70.4 us
    all_gather x1, waiting for transfers between devices, per_device(): gathered_attn = lax.all_gather(normed_attn, 'mp', axis=0, tiled=True)  54.7 us
  transfers between devices with their start and end apart: 9, of which 9 were waited for; matrix products, arithmetic and copies ran while one was open for 9% of the time, Pallas kernels for 0%

profile of v1, /device:TPU:0, one launch (start us, length us, event | category | flops | bytes accessed | tf_op | source)
XLA Modules:
  0.0 1134.9 jit_solution(18147087084932094427)
XLA Ops:
  8.1 1.5 convert_reduce_fusion.1
  9.6 1.6 fusion.28
  14.9 21.4 %all-gather = f32[32,6144]{1,0:T(8,128)S(1)} all-gather(f32[8,6144]{1,0:T(8,128)S(1)} %fusion.78), channel_id=2, replica_groups=mesh['dp'=8,'mp'=4] {'mp'}, dimensions={0}, use_global_device_ids=true | all-gather | bytes 983040 | tf_op jit(solution)/shard_map/all_gather | solution.py:74
  36.5 2.7 fusion.21
  39.9 5.7 convolution_bitcast_fusion
  45.6 12.0 %copy.103 = f32[4,16,16,16,16]{2,1,4,3,0:T(8,128)} copy(f32[4,16,16,16,16]{3,4,1,0,2:T(8,128)} %convolution_bitcast_fusion) | data formatting | bytes 2097152 | tf_op jit(solution)/shard_map/add | solution.py:49
  57.7 7.0 reshape.214
  64.7 54.7 %all-gather.7.cloned.1.call-done = bf16[8,256,1024]{2,1,0:T(8,128)(2,1)} async-done(((bf16[2,256,1024]{2,1,0:T(8,128)(2,1)}), bf16[8,256,1024]{2,1,0:T(8,128)(2,1)}) %all-gather.7.cloned.1.call-update) | async-done | bytes 4194320 | tf_op jit(solution)/shard_map/all_gather | solution.py:109
  119.4 6.1 convert_bitcast_fusion
  126.9 2.9 fusion.83
  129.8 1.7 exponential_reduce_fusion
  131.5 1.5 copy-done.1
  133.0 1.4 convolution_convert_fusion.4
  135.4 3.3 convolution_convert_fusion.1
  138.8 75.4 %reduce-scatter.5.cloned.1.call-done = bf16[2,256,1024]{2,1,0:T(8,128)(2,1)} async-done(((bf16[8,256,1024]{2,1,0:T(8,128)(2,1)}), bf16[2,256,1024]{2,1,0:T(8,128)(2,1)}) %reduce-scatter.5.cloned.1.call-update) | async-done | bytes 1048592 | tf_op jit(solution)/shard_map/reduce_scatter | solution.py:127
  214.2 2.1 fusion.40
  216.3 2.1 multiply_reduce_fusion.3
  218.4 1.6 add_convert_fusion.1
  220.1 2.5 multiply_convert_fusion.5
  222.7 78.7 %all-gather.9.cloned.1.call-done = bf16[8,256,1024]{2,1,0:T(8,128)(2,1)} async-done(((bf16[2,256,1024]{2,1,0:T(8,128)(2,1)}), bf16[8,256,1024]{2,1,0:T(8,128)(2,1)}) %all-gather.9.cloned.1.call-update) | async-done | bytes 4194320 | tf_op jit(solution)/shard_map/all_gather | solution.py:137
  301.5 10.9 fusion.34
  312.4 70.4 %all-gather.11.cloned.1.call-done = bf16[8,256,1024]{2,1,0:T(8,128)(2,1)} async-done(((bf16[2,256,1024]{2,1,0:T(8,128)(2,1)}), bf16[8,256,1024]{2,1,0:T(8,128)(2,1)}) %all-gather.11.cloned.1.call-update) | async-done | bytes 4194320 | tf_op jit(solution)/shard_map/all_gather | solution.py:153
  382.7 12.8 %fusion.6 = bf16[8,256,1024]{2,1,0:T(8,128)(2,1)S(1)} fusion(f32[8,256,1024]{2,1,0:T(8,128)} %fusion.34, bf16[8,256,1024]{2,1,0:T(8,128)(2,1)} %all-gather.11.cloned.1.call-done, bf16[1024,1024]{1,0:T(8,128)(2,1)} %param.19), kind=kOutput, calls=%fused_computation.8 | convolution fusion | flops 4336910336 | bytes 18874368 | tf_op jit(solution)/shard_map/wtd,fd->wtf/dot_general | solution.py:160
  395.5 2.0 copy-done.34
  397.5 7.0 fusion.32
  404.6 143.2 %reduce-scatter.9.cloned.1.call-done = f32[2,256,1024]{2,1,0:T(8,128)} async-done(((f32[8,256,1024]{2,1,0:T(8,128)}), f32[2,256,1024]{2,1,0:T(8,128)}) %reduce-scatter.9.cloned.1.call-update) | async-done | bytes 2097168 | tf_op jit(solution)/shard_map/reduce_scatter | solution.py:166
  547.8 3.3 multiply_reduce_fusion.1
  552.2 1.3 copy-done.6
  553.6 1.4 multiply_convert_fusion.4
  555.1 81.5 %all-gather.13.cloned.1.call-done = bf16[8,256,1024]{2,1,0:T(8,128)(2,1)} async-done(((bf16[2,256,1024]{2,1,0:T(8,128)(2,1)}), bf16[8,256,1024]{2,1,0:T(8,128)(2,1)}) %all-gather.13.cloned.1.call-update) | async-done | bytes 4194320 | tf_op jit(solution)/shard_map/all_gather | solution.py:177
  636.5 3.7 convolution_convert_fusion.3
  640.3 6.0 convolution_convert_fusion.2
  646.3 2.5 multiply_reduce_fusion
  648.8 3.9 convert_reduce_fusion
  652.7 2.4 multiply_convert_fusion.2
  655.1 1.8 multiply_convert_fusion.3
  656.9 2.3 copy.79
  659.1 2.3 copy.77
  661.4 2.3 copy.78
  663.7 7.8 bitcast_convert_fusion
  671.6 11.5 %convolution_convert_fusion = bf16[8,256,1024]{2,1,0:T(8,128)(2,1)} fusion(bf16[1024,1024]{1,0:T(8,128)(2,1)} %param.19, f32[8,256,1024]{2,1,0:T(8,128)} %fusion.34), kind=kOutput, calls=%fused_computation.34 | convolution fusion | flops 4315938816 | bytes 14680064 | tf_op jit(solution)/shard_map/wtf,fd->wtd/dot_general | solution.py:142
  683.4 10.2 convolution_bitcast_fusion.2
  693.6 11.2 convolution_bitcast_fusion.1
  704.8 2.3 convolution_bitcast_fusion.3
  708.4 5.5 fusion.36
  713.8 33.1 %reduce-scatter.11.cloned.1.call-done = bf16[2,256,1024]{2,1,0:T(8,128)(2,1)} async-done(((bf16[8,256,1024]{2,1,0:T(8,128)(2,1)}), bf16[2,256,1024]{2,1,0:T(8,128)(2,1)}) %reduce-scatter.11.cloned.1.call-update) | async-done | bytes 1048592 | tf_op jit(solution)/shard_map/reduce_scatter | solution.py:218
  747.0 1.4 reduce
  748.4 2.1 fusion.29
  750.5 2.7 fusion.27
  753.2 73.9 %reduce-scatter.7.cloned.1.call-done = bf16[2,256,1024]{2,1,0:T(8,128)(2,1)} async-done(((bf16[8,256,1024]{2,1,0:T(8,128)(2,1)}), bf16[2,256,1024]{2,1,0:T(8,128)(2,1)}) %reduce-scatter.7.cloned.1.call-update) | async-done | bytes 1048592 | tf_op jit(solution)/shard_map/reduce_scatter | solution.py:141
  827.2 5.2 fusion.26
  832.5 13.8 %all-gather.1 = bf16[4,2,6144]{2,1,0:T(2,128)(2,1)S(1)} all-gather(bf16[1,2,6144]{2,1,0:T(2,128)(2,1)S(1)} %bitcast.180), channel_id=1, replica_groups=mesh['dp'=8,'mp'=4] {'mp'}, dimensions={0}, use_global_device_ids=true | all-gather | bytes 122880 | tf_op jit(solution)/shard_map/all_gather | solution.py:240
  848.3 1.7 fusion.60
  850.0 3.7 fusion.77
  854.5 6.1 reshape.189
  860.6 6.9 convolution_bitcast_fusion.5
  868.1 25.8 %all-reduce = (f32[6,1024]{1,0:T(8,128)}, f32[4,961]{1,0:T(4,128)}) all-reduce(f32[6,1024]{1,0:T(8,128)S(1)} %reshape.188, f32[4,961]{1,0:T(4,128)S(1)} %reshape.190), channel_id=1, replica_groups=mesh['dp'=8,'mp'=4] {'dp'}, use_global_device_ids=true, to_apply=%region_28.29 | all-reduce | flops 9988 | bytes 79904 | tf_op jit(solution)/shard_map/psum | solution.py:259
  893.9 215.5 %all-reduce.4.cloned.1.call-done = (f32[3,1024,256]{1,2,0:T(8,128)}, f32[256,1024]{1,0:T(8,128)}, f32[1024,1024]{1,0:T(8,128)}, f32[1024,1024]{1,0:T(8,128)}, f3...) async-done(((f32[3,1024,256]{1,2,0:T(8,128)}, f32[256,1024]{1,0:T(8,128)}, f32[1024,1024]{1,0:T(8,128)}, f32[1024,1024]{1,0:T(8,128)}, ...) | async-done | bytes 20160528 | tf_op jit(solution)/shard_map/psum | solution.py:259
  1109.3 3.5 copy.85
  1112.9 2.3 copy.123
  1115.2 5.1 copy.124
  1120.3 2.1 copy.125
  1122.4 1.4 slice-done.3
  1123.8 2.7 copy.126
  (137 shorter events, 16.1 us)
Async XLA Ops:
  7.2 7.2 copy-start
  7.2 112.2 %all-gather.7.cloned.1.call-start = ((), (), s32[]{:S(2)}) async-start(), calls=%async_computation.4 | async-start | bytes 5242880 | tf_op jit(solution)/shard_map/all_gather | solution.py:109
  14.9 24.3 %copy-start.27 = (bf16[4,961]{1,0:T(4,128)(2,1)S(1)}, bf16[4,961]{1,0:T(4,128)(2,1)}, u32[]{:S(2)}) copy-start(bf16[4,961]{1,0:T(4,128)(2,1)} %param.24) | copy-start | bytes 23068
  39.1 175.0 %reduce-scatter.5.cloned.1.call-start = ((), (), s32[]{:S(2)}) async-start(), calls=%async_computation.5 | async-start | bytes 5242880 | tf_op jit(solution)/shard_map/reduce_scatter | solution.py:127
  39.3 0.6 copy-start.25
  57.7 7.0 copy-start.29
  125.5 1.4 copy-start.15
  125.8 4.0 copy-start.7
  125.8 4.0 copy-start.12
  125.8 5.7 copy-start.9
  129.8 3.2 copy-start.1
  133.0 2.4 copy-start.23
  134.4 1.0 copy-start.17
  138.7 162.7 %all-gather.9.cloned.1.call-start = ((), (), s32[]{:S(2)}) async-start(), calls=%async_computation.6 | async-start | bytes 5242880 | tf_op jit(solution)/shard_map/all_gather | solution.py:137
  214.2 4.2 copy-start.2
  214.2 4.2 copy-start.4
  220.1 162.7 %all-gather.11.cloned.1.call-start = ((), (), s32[]{:S(2)}) async-start(), calls=%async_computation.8 | async-start | bytes 5242880 | tf_op jit(solution)/shard_map/all_gather | solution.py:153
  222.7 325.1 %reduce-scatter.9.cloned.1.call-start = ((), (), s32[]{:S(2)}) async-start(), calls=%async_computation.9 | async-start | bytes 10485760 | tf_op jit(solution)/shard_map/reduce_scatter | solution.py:166
  382.7 14.8 %copy-start.33 = (bf16[1024,1024]{1,0:T(8,128)(2,1)S(1)}, bf16[1024,1024]{1,0:T(8,128)(2,1)}, u32[]{:S(2)}) copy-start(bf16[1024,1024]{1,0:T(8,128)(2,1)} %param.18) | copy-start | bytes 6291460
  395.5 2.0 copy-start.34
  404.5 232.0 %all-gather.13.cloned.1.call-start = ((), (), s32[]{:S(2)}) async-start(), calls=%async_computation.10 | async-start | bytes 5242880 | tf_op jit(solution)/shard_map/all_gather | solution.py:177
  547.8 3.3 copy-start.3
  547.8 3.4 copy-start.5
  547.8 3.5 copy-start.14
  551.3 2.3 copy-start.11
  552.2 1.4 copy-start.6
  555.0 191.9 %reduce-scatter.11.cloned.1.call-start = ((), (), s32[]{:S(2)}) async-start(), calls=%async_computation.11 | async-start | bytes 5242880 | tf_op jit(solution)/shard_map/reduce_scatter | solution.py:218
  636.5 9.7 slice-start
  640.3 6.0 slice-start.1
  640.3 6.0 copy-start.10
  648.8 3.9 copy-start.13
  652.7 2.4 copy-start.8
  671.5 155.6 %reduce-scatter.7.cloned.1.call-start = ((), (), s32[]{:S(2)}) async-start(), calls=%async_computation.7 | async-start | bytes 5242880 | tf_op jit(solution)/shard_map/reduce_scatter | solution.py:141
  683.1 426.2 %all-reduce.4.cloned.1.call-start = ((), (), s32[]{:S(2)}) async-start(), calls=%async_computation.12 | async-start | bytes 40321024 | tf_op jit(solution)/shard_map/psum | solution.py:259
  683.4 10.2 copy-start.31
  693.6 11.2 copy-start.18
  693.6 11.2 copy-start.32
  704.8 2.3 copy-start.19
  704.8 2.3 copy-start.20
  704.8 2.3 copy-start.21
  704.8 3.6 copy-start.30
  832.4 15.9 %copy-start.28 = (s32[8]{0:T(128)S(1)}, s32[8]{0:T(128)}, u32[]{:S(2)}) copy-start(s32[8]{0:T(128)} %param.26) | copy-start | bytes 100
  853.7 0.7 copy-start.26
  1115.2 5.1 copy-start.16
  1115.2 7.2 slice-start.2
  1120.3 3.5 slice-start.3
  1123.8 2.7 copy-start.24
  1123.8 3.4 copy-start.22
Sparse Core Ops, SparseCore 0:
  39.3 80.0 all-gather.6
  138.9 75.2 reduce-scatter.4
  220.2 81.2 all-gather.8
  303.5 79.2 all-gather.10
  404.6 143.0 reduce-scatter.8
  555.2 81.3 all-gather.12
  671.6 75.2 reduce-scatter.10
  749.8 77.2 reduce-scatter.6
  853.8 255.4 all-reduce.3
